TPU v7x, 512 devices: a whole 4x8x8 slice. The times are simulated.
512 devices in a mesh: gx: 32 (over z, x), gy: 16 (over y, core).
Axes of the slice: x: 4, y: 8, z: 8, core: 2. Of those that a mesh axis runs over, the one named last changes fastest.
Arguments:
- source: float32 [2048, 256, 128], P('gx', 'gy'), may hold values from -5 to 5
Outputs:
- pressure: float32 [2048, 256, 128], P('gx', 'gy')
All inputs are finite; a program needn't handle non-finite values.
Results may differ from a plain program's by a relative error of at most 0.0003.
Values sent between devices are 32-bit elements; how exact they have to be, the bound alone decides.
A program may use at most 64 MiB of HBM per device.

v0:
```python
import math

import jax
import jax.numpy as jnp
from jax import lax
from jax.sharding import PartitionSpec as P

SCREEN = 32


highest = lax.Precision.HIGHEST


def cosine_table(points, wavenums, places):
    angles = wavenums[:, None] * (2 * places[None, :] + 1) % (4 * points)
    norming = jnp.where(wavenums == 0, math.sqrt(1.0 / points), math.sqrt(2.0 / points)).astype(
        jnp.float32
    )
    return norming[:, None] * jnp.cos(angles.astype(jnp.float32) * (math.pi / (2 * points)))


def eigenvalue(wavenums, points):
    half_angle = jnp.sin(wavenums.astype(jnp.float32) * (math.pi / (2 * points)))
    return 4.0 * half_angle * half_angle


def forward_cosine(received):
    length = received.shape[2]
    width = min(256, length)
    places = jnp.arange(length, dtype=jnp.int32)

    def forward_one_block(index, output):
        offset = index * width
        cos_table = cosine_table(length, offset + jnp.arange(width, dtype=jnp.int32), places)
        piece = jnp.einsum("zyx,kx->zyk", received, cos_table, precision=highest)
        return lax.dynamic_update_slice_in_dim(output, piece, offset, 2)

    return lax.fori_loop(
        0, length // width, forward_one_block, jnp.zeros(received.shape, jnp.float32)
    )


def backward_cosine(solved):
    length = solved.shape[2]
    width = min(256, length)
    waves = jnp.arange(length, dtype=jnp.int32)

    def backward_one_block(index, output):
        offset = index * width
        cos_table = cosine_table(length, waves, offset + jnp.arange(width, dtype=jnp.int32))
        piece = jnp.einsum("zyk,kx->zyx", solved, cos_table, precision=highest)
        return lax.dynamic_update_slice_in_dim(output, piece, offset, 2)

    return lax.fori_loop(
        0, length // width, backward_one_block, jnp.zeros(solved.shape, jnp.float32)
    )


def thomas(rhs_lines, diagonal):

    def forward_step(carry, source_line):
        factor, eliminated = carry
        factor = 1.0 / (diagonal - factor)
        eliminated = (source_line + eliminated) * factor
        return ((factor, eliminated), (factor, eliminated))

    empty_line = jnp.zeros_like(rhs_lines[0])
    unused, (factors, eliminated) = lax.scan(
        forward_step, (empty_line, empty_line), rhs_lines, unroll=8
    )

    def backward_step(pressure_next, inputs_line):
        solved_line = inputs_line[1] + inputs_line[0] * pressure_next
        return (solved_line, solved_line)

    unused_last, solution = lax.scan(
        backward_step, empty_line, (factors, eliminated), reverse=True, unroll=8
    )
    return solution


def shards(source):
    cx_cells, cy_cells, nz_cells = source.shape
    planes = nz_cells // lax.axis_size("gx")
    plane_first = lax.axis_index("gx") * planes
    nz_waves = jnp.arange(nz_cells, dtype=jnp.int32)
    z_table = cosine_table(nz_cells, nz_waves, nz_waves)
    zhat = jnp.einsum("xyz,kz->kyx", source, z_table, precision=highest)
    spectral = forward_cosine(lax.all_to_all(zhat, "gx", split_axis=0, concat_axis=2, tiled=True))
    nx_cells = spectral.shape[2]
    screen_shift = 1.0 / (SCREEN * SCREEN)
    z_eigen = eigenvalue(plane_first + jnp.arange(planes, dtype=jnp.int32), nz_cells)
    columns = lax.all_to_all(spectral, "gy", split_axis=2, concat_axis=1, tiled=True)
    column_count = columns.shape[2]
    column_first = lax.axis_index("gy") * column_count
    x_eigen = eigenvalue(column_first + jnp.arange(column_count, dtype=jnp.int32), nx_cells)
    diagonal = 2.0 + (screen_shift + z_eigen[:, None] + x_eigen[None, :])
    solved_columns = thomas(jnp.moveaxis(columns, 1, 0), diagonal)
    solved = lax.all_to_all(
        jnp.moveaxis(solved_columns, 0, 1), "gy", split_axis=1, concat_axis=2, tiled=True
    )
    physical = backward_cosine(solved)
    regrouped = lax.all_to_all(physical, "gx", split_axis=2, concat_axis=0, tiled=True)
    return jnp.einsum("kyx,kz->xyz", regrouped, z_table, precision=highest)


def solution(mesh):
    return jax.shard_map(
        shards,
        mesh=mesh,
        in_specs=(P("gx", "gy", None),),
        out_specs=P("gx", "gy", None),
        check_vma=False,
    )
```

profile of v0, /device:TPU:1, one launch (start us, length us, event | category | flops | bytes accessed | tf_op | source)
XLA Modules:
  0.0 354.0 jit_solution(14505402717037691400)
XLA Ops:
  3.9 13.7 %all-to-all-start = ((f32[32,1,4096]{2,1,0:T(1,128)}), f32[32,1,4096]{2,1,0:T(1,128)S(1)}, u32[]{:S(2)}, u32[]{:S(2)}) async-start(f32[32,1,4096]{2,1,0:T(1,128)} %reshape.126), calls=%async_computation | async-start | bytes 1048576 | tf_op jit(solution)/shard_map/all_to_all | solution.py:89
  17.6 16.3 %all-to-all-done = f32[32,1,4096]{2,1,0:T(1,128)S(1)} async-done(((f32[32,1,4096]{2,1,0:T(1,128)}), f32[32,1,4096]{2,1,0:T(1,128)S(1)}, u32[]{:S(2)}, u32[]{:S(2)}) %all-to-all-start) | async-done | bytes 524320 | tf_op jit(solution)/shard_map/all_to_all | solution.py:89
  37.8 77.5 %while.67 = (s32[]{:T(128)}, f32[4,16,2048]{2,1,0:T(8,128)S(1)}, f32[4,16,2048]{2,1,0:T(8,128)S(1)}, s32[]{:T(128)}, s32[]{:T(128)}, /*index=5*/s32[]{:T(128)}, s32[]{:T(128)}) while((s32[]{:T(128)}, f32[4,16,2048]{2,1,0:T(8,128)S(1)}, f32[4,16,2048]{2,1,0:T(8,128)S(1)}, s32[]{:T(128)}, s32[]{:T(128)}, /*index=5*/s32[]{:T(128)}, ...), condition=%wide.region_1.2_spmd.clone, body=%wide.region_0.1_spmd.clone.sunk | while | flops 410522624 | bytes 610439 | solution.py:38
  38.2 9.6 %fusion.161 = f32[4,16,2048]{2,1,0:T(8,128)S(1)} fusion(f32[4,16,2048]{2,1,0:T(8,128)S(1)} %get-tuple-element.753, s32[]{:T(128)S(6)} %select_n.174, f32[4,16,2048]{2,1,0:T(8,128)S(1)} %get-tuple-element.761, s32[2048]{0:T(1024)S(1)} %fusion.160, s32[256]{0:T(256)S(1)} %iota_add_fusion.2, f32[256]{0:T(256)S(1)} %compare_select_fusion.3), kind=kOutput, calls=%fused_computation.19.clone.1 | convolution fusion | flops 410517504 | bytes 600068 | tf_op jit(solution)/shard_map/while/body/eval_jaxpr/zyx,kx->zyk/dot_general | solution.py:35
  47.9 9.6 %fusion.161 = f32[4,16,2048]{2,1,0:T(8,128)S(1)} fusion(f32[4,16,2048]{2,1,0:T(8,128)S(1)} %get-tuple-element.753, s32[]{:T(128)S(6)} %select_n.174, f32[4,16,2048]{2,1,0:T(8,128)S(1)} %get-tuple-element.761, s32[2048]{0:T(1024)S(1)} %fusion.160, s32[256]{0:T(256)S(1)} %iota_add_fusion.2, f32[256]{0:T(256)S(1)} %compare_select_fusion.3), kind=kOutput, calls=%fused_computation.19.clone.1 | convolution fusion | flops 410517504 | bytes 600068 | tf_op jit(solution)/shard_map/while/body/eval_jaxpr/zyx,kx->zyk/dot_general | solution.py:35
  57.5 9.6 %fusion.161 = f32[4,16,2048]{2,1,0:T(8,128)S(1)} fusion(f32[4,16,2048]{2,1,0:T(8,128)S(1)} %get-tuple-element.753, s32[]{:T(128)S(6)} %select_n.174, f32[4,16,2048]{2,1,0:T(8,128)S(1)} %get-tuple-element.761, s32[2048]{0:T(1024)S(1)} %fusion.160, s32[256]{0:T(256)S(1)} %iota_add_fusion.2, f32[256]{0:T(256)S(1)} %compare_select_fusion.3), kind=kOutput, calls=%fused_computation.19.clone.1 | convolution fusion | flops 410517504 | bytes 600068 | tf_op jit(solution)/shard_map/while/body/eval_jaxpr/zyx,kx->zyk/dot_general | solution.py:35
  67.2 9.6 %fusion.161 = f32[4,16,2048]{2,1,0:T(8,128)S(1)} fusion(f32[4,16,2048]{2,1,0:T(8,128)S(1)} %get-tuple-element.753, s32[]{:T(128)S(6)} %select_n.174, f32[4,16,2048]{2,1,0:T(8,128)S(1)} %get-tuple-element.761, s32[2048]{0:T(1024)S(1)} %fusion.160, s32[256]{0:T(256)S(1)} %iota_add_fusion.2, f32[256]{0:T(256)S(1)} %compare_select_fusion.3), kind=kOutput, calls=%fused_computation.19.clone.1 | convolution fusion | flops 410517504 | bytes 600068 | tf_op jit(solution)/shard_map/while/body/eval_jaxpr/zyx,kx->zyk/dot_general | solution.py:35
  76.8 9.6 %fusion.161 = f32[4,16,2048]{2,1,0:T(8,128)S(1)} fusion(f32[4,16,2048]{2,1,0:T(8,128)S(1)} %get-tuple-element.753, s32[]{:T(128)S(6)} %select_n.174, f32[4,16,2048]{2,1,0:T(8,128)S(1)} %get-tuple-element.761, s32[2048]{0:T(1024)S(1)} %fusion.160, s32[256]{0:T(256)S(1)} %iota_add_fusion.2, f32[256]{0:T(256)S(1)} %compare_select_fusion.3), kind=kOutput, calls=%fused_computation.19.clone.1 | convolution fusion | flops 410517504 | bytes 600068 | tf_op jit(solution)/shard_map/while/body/eval_jaxpr/zyx,kx->zyk/dot_general | solution.py:35
  86.5 9.6 %fusion.161 = f32[4,16,2048]{2,1,0:T(8,128)S(1)} fusion(f32[4,16,2048]{2,1,0:T(8,128)S(1)} %get-tuple-element.753, s32[]{:T(128)S(6)} %select_n.174, f32[4,16,2048]{2,1,0:T(8,128)S(1)} %get-tuple-element.761, s32[2048]{0:T(1024)S(1)} %fusion.160, s32[256]{0:T(256)S(1)} %iota_add_fusion.2, f32[256]{0:T(256)S(1)} %compare_select_fusion.3), kind=kOutput, calls=%fused_computation.19.clone.1 | convolution fusion | flops 410517504 | bytes 600068 | tf_op jit(solution)/shard_map/while/body/eval_jaxpr/zyx,kx->zyk/dot_general | solution.py:35
  96.1 9.6 %fusion.161 = f32[4,16,2048]{2,1,0:T(8,128)S(1)} fusion(f32[4,16,2048]{2,1,0:T(8,128)S(1)} %get-tuple-element.753, s32[]{:T(128)S(6)} %select_n.174, f32[4,16,2048]{2,1,0:T(8,128)S(1)} %get-tuple-element.761, s32[2048]{0:T(1024)S(1)} %fusion.160, s32[256]{0:T(256)S(1)} %iota_add_fusion.2, f32[256]{0:T(256)S(1)} %compare_select_fusion.3), kind=kOutput, calls=%fused_computation.19.clone.1 | convolution fusion | flops 410517504 | bytes 600068 | tf_op jit(solution)/shard_map/while/body/eval_jaxpr/zyx,kx->zyk/dot_general | solution.py:35
  105.7 9.6 %fusion.161 = f32[4,16,2048]{2,1,0:T(8,128)S(1)} fusion(f32[4,16,2048]{2,1,0:T(8,128)S(1)} %get-tuple-element.753, s32[]{:T(128)S(6)} %select_n.174, f32[4,16,2048]{2,1,0:T(8,128)S(1)} %get-tuple-element.761, s32[2048]{0:T(1024)S(1)} %fusion.160, s32[256]{0:T(256)S(1)} %iota_add_fusion.2, f32[256]{0:T(256)S(1)} %compare_select_fusion.3), kind=kOutput, calls=%fused_computation.19.clone.1 | convolution fusion | flops 410517504 | bytes 600068 | tf_op jit(solution)/shard_map/while/body/eval_jaxpr/zyx,kx->zyk/dot_general | solution.py:35
  123.8 9.5 %all-to-all-start.1 = ((f32[16,1,8192]{2,1,0:T(1,128)}), f32[16,1,8192]{2,1,0:T(1,128)S(1)}, u32[]{:S(2)}, u32[]{:S(2)}) async-start(f32[16,1,8192]{2,1,0:T(1,128)} %reshape.128), calls=%async_computation.1 | async-start | bytes 1048576 | tf_op jit(solution)/shard_map/all_to_all | solution.py:93
  133.5 17.2 %all-to-all-done.1 = f32[16,1,8192]{2,1,0:T(1,128)S(1)} async-done(((f32[16,1,8192]{2,1,0:T(1,128)}), f32[16,1,8192]{2,1,0:T(1,128)S(1)}, u32[]{:S(2)}, u32[]{:S(2)}) %all-to-all-start.1) | async-done | bytes 524320 | tf_op jit(solution)/shard_map/all_to_all | solution.py:93
  160.5 26.0 %while.69 = (s32[]{:T(128)}, f32[4,128]{1,0:T(4,128)S(1)}, f32[4,128]{1,0:T(4,128)S(1)}, f32[32,8,4,128]{3,2,1,0:T(4,128)S(1)}, f32[32,8,4,128]{3,2,1,0:T(4,128)...) while((s32[]{:T(128)}, f32[4,128]{1,0:T(4,128)S(1)}, ...), condition=%wide.region_3.4_spmd.clone, body=%wide.region_2.3_spmd.clone.sunk | while | flops 33288 | bytes 220976 | solution.py:68
  187.5 23.0 %while.70 = (s32[]{:T(128)}, f32[4,128]{1,0:T(4,128)S(1)}, f32[32,8,4,128]{3,2,1,0:T(4,128)}, f32[32,8,4,128]{3,2,1,0:T(4,128)S(1)}, f32[32,8,4,128]{3,2,1,0:T(4...) while((s32[]{:T(128)}, f32[4,128]{1,0:T(4,128)S(1)}, ...), condition=%wide.region_5.6_spmd.clone, body=%wide.region_4.5_spmd.clone.sunk | while | flops 8714 | bytes 114971 | solution.py:76
  210.5 12.1 %all-to-all-start.2 = ((f32[4,256,128]{2,0,1:T(4,128)}), f32[4,256,128]{2,0,1:T(4,128)S(1)}, u32[]{:S(2)}, u32[]{:S(2)}) async-start(f32[4,256,128]{2,0,1:T(4,128)} %bitcast.11), calls=%async_computation.2 | async-start | bytes 1048576 | tf_op jit(solution)/shard_map/all_to_all | solution.py:99
  222.6 16.5 %all-to-all-done.2 = f32[4,256,128]{2,0,1:T(4,128)S(1)} async-done(((f32[4,256,128]{2,0,1:T(4,128)}), f32[4,256,128]{2,0,1:T(4,128)S(1)}, u32[]{:S(2)}, u32[]{:S(2)}) %all-to-all-start.2) | async-done | bytes 524320 | tf_op jit(solution)/shard_map/all_to_all | solution.py:99
  239.6 73.0 %while.68 = (s32[]{:T(128)}, f32[4,16,2048]{2,1,0:T(8,128)S(1)}, f32[4,16,2048]{2,1,0:T(8,128)S(1)}, s32[]{:T(128)}, s32[]{:T(128)}, /*index=5*/s32[]{:T(128)}, s32[]{:T(128)}) while((s32[]{:T(128)}, f32[4,16,2048]{2,1,0:T(8,128)S(1)}, f32[4,16,2048]{2,1,0:T(8,128)S(1)}, s32[]{:T(128)}, s32[]{:T(128)}, ...), condition=%wide.region_7.8_spmd.clone.clone, body=%wide.region_6.7_spmd.clone.clone.sunk | while | flops 410522368 | bytes 608387 | solution.py:54
  248.7 9.1 %fusion.165 = f32[4,16,2048]{2,1,0:T(8,128)S(1)} fusion(f32[4,16,2048]{2,1,0:T(8,128)S(1)} %get-tuple-element.870, s32[]{:T(128)S(6)} %select_n.177, f32[4,16,2048]{2,1,0:T(8,128)S(1)} %get-tuple-element.878, s32[256]{0:T(256)S(1)} %multiply_add_fusion.3, f32[2048]{0:T(1024)S(1)} %fusion.164), kind=kOutput, calls=%fused_computation.50.clone.1 | convolution fusion | flops 410517504 | bytes 599044 | tf_op jit(solution)/shard_map/while/body/eval_jaxpr/zyk,kx->zyx/dot_general | solution.py:51
  257.9 9.1 %fusion.165 = f32[4,16,2048]{2,1,0:T(8,128)S(1)} fusion(f32[4,16,2048]{2,1,0:T(8,128)S(1)} %get-tuple-element.870, s32[]{:T(128)S(6)} %select_n.177, f32[4,16,2048]{2,1,0:T(8,128)S(1)} %get-tuple-element.878, s32[256]{0:T(256)S(1)} %multiply_add_fusion.3, f32[2048]{0:T(1024)S(1)} %fusion.164), kind=kOutput, calls=%fused_computation.50.clone.1 | convolution fusion | flops 410517504 | bytes 599044 | tf_op jit(solution)/shard_map/while/body/eval_jaxpr/zyk,kx->zyx/dot_general | solution.py:51
  276.1 9.1 %fusion.165 = f32[4,16,2048]{2,1,0:T(8,128)S(1)} fusion(f32[4,16,2048]{2,1,0:T(8,128)S(1)} %get-tuple-element.870, s32[]{:T(128)S(6)} %select_n.177, f32[4,16,2048]{2,1,0:T(8,128)S(1)} %get-tuple-element.878, s32[256]{0:T(256)S(1)} %multiply_add_fusion.3, f32[2048]{0:T(1024)S(1)} %fusion.164), kind=kOutput, calls=%fused_computation.50.clone.1 | convolution fusion | flops 410517504 | bytes 599044 | tf_op jit(solution)/shard_map/while/body/eval_jaxpr/zyk,kx->zyx/dot_general | solution.py:51
  294.4 9.1 %fusion.165 = f32[4,16,2048]{2,1,0:T(8,128)S(1)} fusion(f32[4,16,2048]{2,1,0:T(8,128)S(1)} %get-tuple-element.870, s32[]{:T(128)S(6)} %select_n.177, f32[4,16,2048]{2,1,0:T(8,128)S(1)} %get-tuple-element.878, s32[256]{0:T(256)S(1)} %multiply_add_fusion.3, f32[2048]{0:T(1024)S(1)} %fusion.164), kind=kOutput, calls=%fused_computation.50.clone.1 | convolution fusion | flops 410517504 | bytes 599044 | tf_op jit(solution)/shard_map/while/body/eval_jaxpr/zyk,kx->zyx/dot_general | solution.py:51
  303.5 9.1 %fusion.165 = f32[4,16,2048]{2,1,0:T(8,128)S(1)} fusion(f32[4,16,2048]{2,1,0:T(8,128)S(1)} %get-tuple-element.870, s32[]{:T(128)S(6)} %select_n.177, f32[4,16,2048]{2,1,0:T(8,128)S(1)} %get-tuple-element.878, s32[256]{0:T(256)S(1)} %multiply_add_fusion.3, f32[2048]{0:T(1024)S(1)} %fusion.164), kind=kOutput, calls=%fused_computation.50.clone.1 | convolution fusion | flops 410517504 | bytes 599044 | tf_op jit(solution)/shard_map/while/body/eval_jaxpr/zyk,kx->zyx/dot_general | solution.py:51
  320.4 21.3 %all_to_all.72 = f32[32,1,4096]{2,1,0:T(1,128)S(1)} all-to-all(f32[32,1,4096]{2,1,0:T(1,128)S(1)} %reshape.130), channel_id=1, replica_groups=mesh['gx'=32,'gy'=16] {'gx'}, dimensions={0} | all-to-all | bytes 1048576 | tf_op jit(solution)/shard_map/all_to_all | solution.py:103
  (816 shorter events, 121.3 us)
Async XLA Ops:
  0.0 1.0 copy-start
  3.9 30.0 %all-to-all-start = ((f32[32,1,4096]{2,1,0:T(1,128)}), f32[32,1,4096]{2,1,0:T(1,128)S(1)}, u32[]{:S(2)}, u32[]{:S(2)}) async-start(f32[32,1,4096]{2,1,0:T(1,128)} %reshape.126), calls=%async_computation | async-start | bytes 1048576 | tf_op jit(solution)/shard_map/all_to_all | solution.py:89
  123.8 26.8 %all-to-all-start.1 = ((f32[16,1,8192]{2,1,0:T(1,128)}), f32[16,1,8192]{2,1,0:T(1,128)S(1)}, u32[]{:S(2)}, u32[]{:S(2)}) async-start(f32[16,1,8192]{2,1,0:T(1,128)} %reshape.128), calls=%async_computation.1 | async-start | bytes 1048576 | tf_op jit(solution)/shard_map/all_to_all | solution.py:93
  210.5 28.6 %all-to-all-start.2 = ((f32[4,256,128]{2,0,1:T(4,128)}), f32[4,256,128]{2,0,1:T(4,128)S(1)}, u32[]{:S(2)}, u32[]{:S(2)}) async-start(f32[4,256,128]{2,0,1:T(4,128)} %bitcast.11), calls=%async_computation.2 | async-start | bytes 1048576 | tf_op jit(solution)/shard_map/all_to_all | solution.py:99
where the time goes:
time: 359 us; the launch traced here: 354 us
  matrix products  151 us (42%)
  local copies, waits for them, and re-layouts  64.1 us (18%)
  waiting for transfers between devices  50 us (14%)
  starting transfers between devices  35.4 us (10%)
  other arithmetic  28.3 us (8%)
  blocking collectives  21.3 us (6%)
    dot_general x8, matrix products, forward_one_block(): piece = jnp.einsum('zyx,kx->zyk', received, cos_table, precision=highest)  76.7 us
    dot_general x8, matrix products, backward_one_block(): piece = jnp.einsum('zyk,kx->zyx', solved, cos_table, precision=highest)  72.7 us
    unnamed x8, local copies, waits for them, and re-layouts  21.6 us
    all_to_all x1, blocking collectives, shards(): lax.all_to_all(physical, 'gx', split_axis=2, concat_axis=0, tiled=True)  21.3 us
    dynamic_update_slice x64, local copies, waits for them, and re-layouts, thomas(): lax.scan(forward_step, (empty_line, empty_line), rhs_lines, unroll=8)  20.1 us
    while x256, other arithmetic  19.5 us
    all_to_all x1, waiting for transfers between devices, shards(): lax.all_to_all(spectral, 'gy', split_axis=2, concat_axis=1, tiled=True)  17.2 us
    all_to_all x1, waiting for transfers between devices, shards(): lax.all_to_all(jnp.moveaxis(solved_columns, 0, 1), 'gy', split_axis=1, co...  16.5 us
  transfers between devices with their start and end apart: 3, of which 3 were waited for; matrix products, arithmetic and copies ran while one was open for 0% of the time, Pallas kernels for 0%

commit v1 on v0

v1 whole, which is shorter than its diff:
```python
import functools
import math

import jax
import jax.numpy as jnp
import ml_dtypes
import numpy as np
from jax import lax
from jax.experimental import pallas as pl
from jax.experimental.pallas import tpu as pltpu
from jax.sharding import PartitionSpec as P

SCREEN = 32
X_CHIPS = 8
CHUNKS = 2
MESH = pl.DeviceIdType.MESH
f32, bf16 = jnp.float32, jnp.bfloat16


def halves(table):
    high = table.astype(ml_dtypes.bfloat16)
    low = (table - high.astype(np.float64)).astype(ml_dtypes.bfloat16)
    return high, low


def z_tables(nz, gy):
    waves, places = np.arange(nz)[:, None], np.arange(nz)[None, :]
    norm = np.where(waves == 0, math.sqrt(1.0 / nz), math.sqrt(2.0 / nz))
    cosines = norm * np.cos(np.pi * ((waves * (2 * places + 1)) % (4 * nz)) / (2 * nz))
    group = nz // gy // CHUNKS
    blocks = cosines.reshape(gy, CHUNKS, group, nz)
    table = np.zeros((CHUNKS, gy, 2, group, 2, nz))
    for bit in range(2):
        table[:, :, bit, :, bit, :] = blocks.transpose(1, 0, 2, 3)
    return halves(table.reshape(CHUNKS, gy * 2 * group, 2 * nz))


def y_tables(ny, gy):
    line = np.arange(1, ny + 1)
    sines = math.sqrt(2.0 / (ny + 1)) * np.sin(
        np.pi * ((line[:, None] * line[None, :]) % (2 * (ny + 1))) / (ny + 1)
    )
    quads = sines.reshape(gy, ny // gy // 4, 2, 2, ny)
    return halves(quads.transpose(3, 2, 0, 1, 4).reshape(ny, ny))


def line_tables(ny, nz, gy):
    q, m = np.arange(ny), np.arange(nz)
    shift = (
        1.0 / (SCREEN * SCREEN)
        + 4.0 * np.sin(np.pi * (q[:, None] + 1) / (2 * (ny + 1))) ** 2
        + 4.0 * np.sin(np.pi * m[None, :] / (2 * nz)) ** 2
    )
    root = np.sqrt(shift * (1.0 + shift / 4.0))
    ratio = 1.0 / (1.0 + shift / 2.0 + root)
    both = np.stack([ratio, 0.5 / root])
    group = nz // gy // CHUNKS
    both = both.reshape(2, 2, ny // 2, gy, CHUNKS, group)
    both = both.transpose(3, 4, 0, 1, 5, 2)
    return both.reshape(gy, CHUNKS, 2, 2 * group, ny // 2).astype(np.float32)


def split(value):
    high = value.astype(bf16)
    return high, (value - high.astype(f32)).astype(bf16)


def product(left, right, dims):
    def dot(a, b):
        return lax.dot_general(a, b, (dims, ((), ())), preferred_element_type=f32)

    return dot(left[0], right[0]) + (dot(left[1], right[0]) + dot(left[0], right[1]))


def kernel(
    gx, gy, x_chips, lx, ly, nz, ny,
    f_ref, c_hi_hbm, c_lo_hbm, s_hi_hbm, s_lo_hbm, lines_hbm,
    o_ref,
    c_hi, c_lo, s_hi, s_lo, lines,
    g_hi, g_lo, out_fwd, in_fwd, wave, powers, sums_up, sums_down, solved, out_bwd, in_bwd, total,
    ends, ends_x, tops, tops_z,
    table_sem, fwd_send, fwd_recv, bwd_send, bwd_recv, x_send, x_recv, z_send, z_recv,
):
    z_chips, y_chips = gx // x_chips, gy // 2
    quads = ly // 4
    group = nz // gy // CHUNKS
    rows = 2 * group
    block = quads * rows
    half = gy * quads
    ql = ny // 2

    gxi, gyi = lax.axis_index("gx"), lax.axis_index("gy")
    zi, xi = gxi // x_chips, lax.rem(gxi, x_chips)
    yi, core = gyi // 2, lax.rem(gyi, 2)

    def y_peer(sign, dy, dc):
        chip = lax.rem(yi + sign * dy + y_chips, y_chips)
        return chip * 2 + lax.rem(core + dc, 2)

    order = sorted(range(y_chips), key=lambda d: (-min(d, y_chips - d), d))
    y_moves = [(dy, dc) for dy in order for dc in range(2) if (dy, dc) != (0, 0)]
    x_order = sorted(range(1, x_chips), key=lambda d: (-min(d, x_chips - d), d))

    def x_peer(sign, d):
        return zi * x_chips + lax.rem(xi + sign * d + x_chips, x_chips)

    def z_peer(sign, d):
        return lax.rem(zi + sign * d + z_chips, z_chips) * x_chips + xi

    barrier = pltpu.get_barrier_semaphore()
    for dy, dc in y_moves:
        pl.semaphore_signal(
            barrier, inc=1, device_id=(gxi, y_peer(1, dy, dc)), device_id_type=MESH
        )
    for d in x_order:
        pl.semaphore_signal(barrier, inc=1, device_id=(x_peer(1, d), gyi), device_id_type=MESH)
    for d in range(1, z_chips):
        pl.semaphore_signal(barrier, inc=1, device_id=(z_peer(1, d), gyi), device_id_type=MESH)

    loads = [
        pltpu.make_async_copy(source, target, table_sem.at[i])
        for i, (source, target) in enumerate(
            [
                (c_hi_hbm, c_hi),
                (c_lo_hbm, c_lo),
                (s_hi_hbm, s_hi),
                (s_lo_hbm, s_lo),
                (lines_hbm.at[gyi], lines),
            ]
        )
    ]
    for load in loads:
        load.start()

    for t in range(quads):
        cells = [[f_ref[pl.ds(4 * t + 2 * b1 + b0, lx, stride=ly), :] for b1 in range(2)]
                 for b0 in range(2)]
        spread = jnp.concatenate([jnp.concatenate(row, axis=1) for row in cells], axis=0)
        high, low = split(spread)
        g_hi[t] = high
        g_lo[t] = low
    for load in loads:
        load.wait()

    def block_of(index):
        return pl.ds(pl.multiple_of(index * block, block), block)

    def z_forward(c):
        for t in range(quads):
            piece = product((c_hi[c], c_lo[c]), (g_hi[t], g_lo[t]), ((1,), (1,)))
            for j in range(gy):
                out_fwd[c, j * block + t * rows : j * block + (t + 1) * rows, :] = piece[
                    j * rows : (j + 1) * rows, :
                ]

    def y_copies(c, out, into, send, recv):
        sends, arrivals = [], []
        for i, (dy, dc) in enumerate(y_moves):
            peer, source = y_peer(1, dy, dc), y_peer(-1, dy, dc)
            for copies, src, dst in ((sends, peer, gyi), (arrivals, source, source)):
                copies.append(
                    pltpu.make_async_remote_copy(
                        src_ref=out.at[c, block_of(src)],
                        dst_ref=into.at[c, block_of(dst)],
                        send_sem=send.at[c, i],
                        recv_sem=recv.at[c, i],
                        device_id=(gxi, peer),
                        device_id_type=MESH,
                    )
                )
        return sends, arrivals

    def exchange(c, out, into, send, recv):
        sends, arrivals = y_copies(c, out, into, send, recv)
        for copy in sends:
            copy.start()
        into[c, block_of(gyi), :] = out[c, block_of(gyi), :]
        return sends, arrivals

    z_forward(0)
    pl.semaphore_wait(barrier, len(y_moves) + x_chips - 1 + z_chips - 1)
    fwd = [exchange(0, out_fwd, in_fwd, fwd_send, fwd_recv)]
    for c in range(1, CHUNKS):
        z_forward(c)
        fwd.append(exchange(c, out_fwd, in_fwd, fwd_send, fwd_recv))

    for c in range(CHUNKS):
        ratio = lines[c, 0]
        power = jnp.ones_like(ratio)
        for b in range(lx):
            powers[c, b] = power
            power = power * ratio

    def y_forward(c):
        for copy in fwd[c][1]:
            copy.wait_recv()
        tall = []
        for m in range(group):
            cells = jnp.concatenate(
                [in_fwd[c, pl.ds(b1 * group + m, half, stride=rows), :] for b1 in range(2)], axis=0
            ).T
            tall.append(jnp.concatenate([cells[:lx], cells[lx:]], axis=1))
        spectral = product(split(jnp.concatenate(tall, axis=0)), (s_hi[...], s_lo[...]),
                           ((1,), (0,)))
        for h in range(2):
            wave[c, h * group * lx : (h + 1) * group * lx, :] = spectral[:, h * ql : (h + 1) * ql]

    def small_copies(c, out, into, slot, send, recv, distances, peer_of, source_slot):
        sends, arrivals = [], []
        for i, d in enumerate(distances):
            for copies, dst in ((sends, slot), (arrivals, source_slot(d))):
                copies.append(
                    pltpu.make_async_remote_copy(
                        src_ref=out.at[c],
                        dst_ref=into.at[c, dst],
                        send_sem=send.at[c, i],
                        recv_sem=recv.at[c, i],
                        device_id=(peer_of(1, d), gyi),
                        device_id_type=MESH,
                    )
                )
        return sends, arrivals

    def line(ref, c, b):
        return ref[c, pl.ds(b, rows, stride=lx), :]

    def x_ends(c):
        left = [jnp.zeros((rows, ql), f32) for _ in range(4)]
        right = list(left)
        for b in range(lx):
            value = line(wave, c, b)
            left[b % 4] += value * powers[c, b]
            right[b % 4] += value * powers[c, lx - 1 - b]
        ends[c, 0] = (left[0] + left[1]) + (left[2] + left[3])
        ends[c, 1] = (right[0] + right[1]) + (right[2] + right[3])
        sends, arrivals = small_copies(
            c, ends, ends_x, xi, x_send, x_recv, x_order, x_peer,
            lambda d: lax.rem(xi - d + x_chips, x_chips),
        )
        for copy in sends:
            copy.start()
        ends_x[c, xi] = ends[c]
        return sends, arrivals

    def x_local(c):
        ratio = lines[c, 0]
        up = jnp.zeros((rows, ql), f32)
        down = up
        for b in range(lx):
            up = ratio * up + line(wave, c, b)
            sums_up[c, b] = up
            d = lx - 1 - b
            down = ratio * down
            sums_down[c, d] = down
            down = down + line(wave, c, d)

    def x_group(c, copies):
        for copy in copies[1]:
            copy.wait_recv()
        span = powers[c, lx - 1] * lines[c, 0]
        left = ends_x[c, x_chips - 1, 0]
        right = ends_x[c, 0, 1]
        for i in range(1, x_chips):
            left = span * left + ends_x[c, x_chips - 1 - i, 0]
            right = span * right + ends_x[c, i, 1]
        tops[c, 0] = left
        tops[c, 1] = right
        sends, arrivals = small_copies(
            c, tops, tops_z, zi, z_send, z_recv, range(1, z_chips), z_peer,
            lambda d: lax.rem(zi - d + z_chips, z_chips),
        )
        for copy in sends:
            copy.start()
        tops_z[c, zi] = tops[c]
        return sends, arrivals

    def arriving(span, count, place, parts, left_start, right_start):
        right = right_start
        left = left_start
        for i in range(count):
            left = jnp.where(i < place, span * left + parts(i, 1), left)
            o = count - 1 - i
            right = jnp.where(o > place, span * right + parts(o, 0), right)
        return left, right

    def x_finish(c, copies):
        ratio, scale = lines[c, 0], lines[c, 1]
        span = powers[c, lx - 1] * ratio
        wide = span
        for _ in range(x_chips - 1):
            wide = wide * span
        whole = wide
        for _ in range(z_chips - 1):
            whole = whole * wide
        for copy in copies[1]:
            copy.wait_recv()
        left = tops_z[c, z_chips - 1, 0]
        right = tops_z[c, 0, 1]
        for i in range(1, z_chips):
            left = wide * left + tops_z[c, z_chips - 1 - i, 0]
            right = wide * right + tops_z[c, i, 1]
        closing = 1.0 / (1.0 - whole * whole)
        first = (left + whole * right) * closing
        last = (right + whole * left) * closing
        first, last = arriving(wide, z_chips, zi, lambda i, s: tops_z[c, i, s], first, last)
        first, last = arriving(span, x_chips, xi, lambda i, s: ends_x[c, i, s], first, last)
        first = first * (ratio * scale)
        last = last * (ratio * scale)
        for b in range(lx):
            solved[c, pl.ds(b, rows, stride=lx), :] = (
                scale * (sums_up[c, b] + sums_down[c, b])
                + first * powers[c, b]
                + last * powers[c, lx - 1 - b]
            )

    def y_backward(c):
        flat = group * lx
        lanes = jnp.concatenate([solved[c, h * flat : (h + 1) * flat, :] for h in range(2)], axis=1)
        cells = product(split(lanes), (s_hi[...], s_lo[...]), ((1,), (1,)))
        for m in range(group):
            part = cells[m * lx : (m + 1) * lx]
            part = jnp.concatenate([part[:, : ny // 2], part[:, ny // 2 :]], axis=0).T
            for b1 in range(2):
                out_bwd[c, pl.ds(b1 * group + m, half, stride=rows), :] = part[
                    b1 * half : (b1 + 1) * half
                ]
        return exchange(c, out_bwd, in_bwd, bwd_send, bwd_recv)

    def z_backward(c, copies):
        for copy in copies[1]:
            copy.wait_recv()
        for t in range(quads):
            waves = jnp.concatenate(
                [in_bwd[c, j * block + t * rows : j * block + (t + 1) * rows, :]
                 for j in range(gy)], axis=0,
            ).T
            cells = product(split(waves), (c_hi[c], c_lo[c]), ((1,), (0,)))
            if c > 0:
                cells = cells + total[t]
            if c < CHUNKS - 1:
                total[t] = cells
            else:
                for b0 in range(2):
                    for b1 in range(2):
                        o_ref[pl.ds(4 * t + 2 * b1 + b0, lx, stride=ly), :] = cells[
                            b0 * lx : (b0 + 1) * lx, b1 * nz : (b1 + 1) * nz
                        ]

    assert CHUNKS == 2
    y_forward(0)
    x_copies = [x_ends(0)]
    x_local(0)
    y_forward(1)
    x_copies.append(x_ends(1))
    z_copies = [x_group(0, x_copies[0])]
    x_local(1)
    x_finish(0, z_copies[0])
    bwd = [y_backward(0)]
    z_copies.append(x_group(1, x_copies[1]))
    x_finish(1, z_copies[1])
    bwd.append(y_backward(1))
    z_backward(0, bwd[0])
    z_backward(1, bwd[1])
    for sends, _ in fwd + x_copies + z_copies + bwd:
        for copy in sends:
            copy.wait_send()


def solve(gx, gy, x_chips, source):
    lx, ly, nz = source.shape
    ny = ly * gy
    z_chips = gx // x_chips
    group = nz // gy // CHUNKS
    rows, ql = 2 * group, ny // 2
    c_hi, c_lo = z_tables(nz, gy)
    s_hi, s_lo = y_tables(ny, gy)
    lines = line_tables(ny, nz, gy)
    buffer = pltpu.VMEM((CHUNKS, gy * (ly // 4) * rows, 2 * lx), f32)
    spectral = pltpu.VMEM((CHUNKS, rows * lx, ql), f32)
    stack = pltpu.VMEM((CHUNKS, lx, rows, ql), f32)
    quad = pltpu.VMEM((ly // 4, 2 * lx, 2 * nz), bf16)
    dma = pltpu.SemaphoreType.DMA
    scratch = [
        pltpu.VMEM(c_hi.shape, bf16), pltpu.VMEM(c_lo.shape, bf16),
        pltpu.VMEM(s_hi.shape, bf16), pltpu.VMEM(s_lo.shape, bf16),
        pltpu.VMEM(lines.shape[1:], f32),
        quad, quad, buffer, buffer, spectral, stack, stack, stack, spectral, buffer, buffer,
        pltpu.VMEM((ly // 4, 2 * lx, 2 * nz), f32),
        pltpu.VMEM((CHUNKS, 2, rows, ql), f32),
        pltpu.VMEM((CHUNKS, x_chips, 2, rows, ql), f32),
        pltpu.VMEM((CHUNKS, 2, rows, ql), f32),
        pltpu.VMEM((CHUNKS, z_chips, 2, rows, ql), f32),
        dma((5,)),
        dma((CHUNKS, gy - 1)), dma((CHUNKS, gy - 1)), dma((CHUNKS, gy - 1)), dma((CHUNKS, gy - 1)),
        dma((CHUNKS, x_chips - 1)), dma((CHUNKS, x_chips - 1)),
        dma((CHUNKS, z_chips - 1)), dma((CHUNKS, z_chips - 1)),
    ]
    vmem, anywhere = pl.BlockSpec(memory_space=pltpu.VMEM), pl.BlockSpec(memory_space=pl.ANY)
    pressure = pl.pallas_call(
        functools.partial(kernel, gx, gy, x_chips, lx, ly, nz, ny),
        out_shape=jax.ShapeDtypeStruct((lx * ly, nz), f32),
        in_specs=[vmem] + [anywhere] * 5,
        out_specs=vmem,
        scratch_shapes=scratch,
        compiler_params=pltpu.CompilerParams(collective_id=0, has_side_effects=True),
    )(source.reshape(lx * ly, nz), c_hi, c_lo, s_hi, s_lo, lines)
    return pressure.reshape(lx, ly, nz)


def solution(mesh):
    gx, gy = mesh.shape["gx"], mesh.shape["gy"]
    return jax.shard_map(
        functools.partial(solve, gx, gy, X_CHIPS),
        mesh=mesh,
        in_specs=(P("gx", "gy", None),),
        out_specs=P("gx", "gy", None),
        check_vma=False,
    )
```

time: 359 us -> 53.2 us (0.15); the launches traced: 354 us -> 52.9 us
  matrix products: 151 us -> 0 us
  local copies, waits for them, and re-layouts: 64.1 us -> 1.87 us
  Pallas kernels: 0 us -> 51.1 us
  waiting for transfers between devices: 50 us -> 0 us
  starting transfers between devices: 35.4 us -> 0 us
  other arithmetic: 28.3 us -> 0 us
  blocking collectives: 21.3 us -> 0 us
    dot_general x17 -> x0, matrix products: 150 us -> none  [the longest x8 76.7 us: forward_one_block(): piece = jnp.einsum('zyx,kx->zyk', received, cos_table, precision=highest)]
    pallas_call x0 -> x1, Pallas kernels: none -> 51.1 us  [solve(): pl.pallas_call(functools.partial(kernel, gx, gy, x_chips, lx, ly, nz, ny)...]
    all_to_all x3 -> x0, waiting for transfers between devices: 50 us -> none  [the longest x1 17.2 us: shards(): lax.all_to_all(spectral, 'gy', split_axis=2, concat_axis=1, tiled=True)]
    all_to_all x3 -> x0, starting transfers between devices: 35.4 us -> none  [the longest x1 13.7 us: shards(): lax.all_to_all(zhat, 'gx', split_axis=0, concat_axis=2, tiled=True)]
    all_to_all x1 -> x0, blocking collectives: 21.3 us -> none  [shards(): lax.all_to_all(physical, 'gx', split_axis=2, concat_axis=0, tiled=True)]
    dynamic_update_slice x64 -> x0, local copies, waits for them, and re-layouts: 20.1 us -> none  [thomas(): lax.scan(forward_step, (empty_line, empty_line), rhs_lines, unroll=8)]
    unnamed x8 -> x1, local copies, waits for them, and re-layouts: 21.6 us -> 1.87 us
    while x256 -> x0, other arithmetic: 19.5 us -> none
  transfers between devices with their start and end apart: 3 -> 0, of which waited for: 3 -> 0; matrix products, arithmetic and copies ran while one was open for 0% -> 0% of each run, Pallas kernels for 0% -> 0%
where the time goes in v1:
time: 53.2 us; the launch traced here: 52.9 us
  Pallas kernels  51.1 us (96%)
  local copies, waits for them, and re-layouts  1.87 us (4%)
    pallas_call x1, Pallas kernels, solve(): pl.pallas_call(functools.partial(kernel, gx, gy, x_chips, lx, ly, nz, ny)...  51.1 us
    unnamed x1, local copies, waits for them, and re-layouts  1.87 us

profile of v1, /device:TPU:1, one launch (start us, length us, event | category | flops | bytes accessed | tf_op | source)
XLA Modules:
  0.0 52.9 jit_solution(7728420068621655291)
XLA Ops:
  0.0 51.1 %shard_map.64 = f32[1024,128]{1,0:T(8,128)} custom-call(f32[1024,128]{1,0:T(8,128)} %bitcast.3, bf16[2,128,256]{2,1,0:T(8,128)(2,1)} %constant.10.clone.c_hi_hbm, bf16[2,128,256]{2,1,0:T(8,128)(2,1)} %constant.11.clone.c_lo_hbm, bf16[256,256]{1,0:T(8,128)(2,1)} %constant.12.clone.s_hi_hbm, bf16[256,256]{1,0:T(8,128)(2,1)} %constant.13.clone.s_lo_hbm, ...), custom_call_target="tpu_custom_call" | custom-call | tf_op jit(solution)/shard_map/pallas_call | solution.py:399
  51.1 1.9 %copy.8 = f32[64,16,128]{2,1,0:T(8,128)} copy(f32[64,16,128]{2,1,0:T(8,128)} %bitcast.2) | data formatting | bytes 1048576

commit v2 on v1

--- a/solution.py
+++ b/solution.py
@@ -12,7 +12,8 @@
 
 SCREEN = 32
 X_CHIPS = 8
-CHUNKS = 2
+CHUNKS = 4
+TILE = 8
 MESH = pl.DeviceIdType.MESH
 f32, bf16 = jnp.float32, jnp.bfloat16
 
@@ -28,20 +29,21 @@
     norm = np.where(waves == 0, math.sqrt(1.0 / nz), math.sqrt(2.0 / nz))
     cosines = norm * np.cos(np.pi * ((waves * (2 * places + 1)) % (4 * nz)) / (2 * nz))
     group = nz // gy // CHUNKS
+    sub = TILE // group
     blocks = cosines.reshape(gy, CHUNKS, group, nz)
-    table = np.zeros((CHUNKS, gy, 2, group, 2, nz))
-    for bit in range(2):
-        table[:, :, bit, :, bit, :] = blocks.transpose(1, 0, 2, 3)
-    return halves(table.reshape(CHUNKS, gy * 2 * group, 2 * nz))
-
-
-def y_tables(ny, gy):
+    table = np.zeros((CHUNKS, gy, sub, group, sub, nz))
+    for s in range(sub):
+        table[:, :, s, :, s, :] = blocks.transpose(1, 0, 2, 3)
+    return halves(table.reshape(CHUNKS, gy * TILE, sub * nz))
+
+
+def y_tables(ny, gy, sub):
     line = np.arange(1, ny + 1)
     sines = math.sqrt(2.0 / (ny + 1)) * np.sin(
         np.pi * ((line[:, None] * line[None, :]) % (2 * (ny + 1))) / (ny + 1)
     )
-    quads = sines.reshape(gy, ny // gy // 4, 2, 2, ny)
-    return halves(quads.transpose(3, 2, 0, 1, 4).reshape(ny, ny))
+    cells = sines.reshape(gy, ny // gy // (2 * sub), sub, 2, ny)
+    return halves(cells.transpose(3, 2, 0, 1, 4).reshape(ny, ny))
 
 
 def line_tables(ny, nz, gy):
@@ -74,19 +76,20 @@
 
 def kernel(
     gx, gy, x_chips, lx, ly, nz, ny,
-    f_ref, c_hi_hbm, c_lo_hbm, s_hi_hbm, s_lo_hbm, lines_hbm,
+    f_hbm, c_hi_hbm, c_lo_hbm, s_hi_hbm, s_lo_hbm, lines_hbm,
     o_ref,
-    c_hi, c_lo, s_hi, s_lo, lines,
+    f_ref, c_hi, c_lo, s_hi, s_lo, lines,
     g_hi, g_lo, out_fwd, in_fwd, wave, powers, sums_up, sums_down, solved, out_bwd, in_bwd, total,
     ends, ends_x, tops, tops_z,
     table_sem, fwd_send, fwd_recv, bwd_send, bwd_recv, x_send, x_recv, z_send, z_recv,
 ):
     z_chips, y_chips = gx // x_chips, gy // 2
-    quads = ly // 4
     group = nz // gy // CHUNKS
+    sub = TILE // group
+    steps = ly // (2 * sub)
     rows = 2 * group
-    block = quads * rows
-    half = gy * quads
+    block = steps * TILE
+    part = gy * steps
     ql = ny // 2
 
     gxi, gyi = lax.axis_index("gx"), lax.axis_index("gy")
@@ -117,40 +120,37 @@
     for d in range(1, z_chips):
         pl.semaphore_signal(barrier, inc=1, device_id=(z_peer(1, d), gyi), device_id_type=MESH)
 
-    loads = [
-        pltpu.make_async_copy(source, target, table_sem.at[i])
-        for i, (source, target) in enumerate(
-            [
-                (c_hi_hbm, c_hi),
-                (c_lo_hbm, c_lo),
-                (s_hi_hbm, s_hi),
-                (s_lo_hbm, s_lo),
-                (lines_hbm.at[gyi], lines),
-            ]
-        )
+    def load(index, source, target):
+        copy = pltpu.make_async_copy(source, target, table_sem.at[index])
+        copy.start()
+        return copy
+
+    first_loads = [load(0, f_hbm, f_ref), load(1, c_hi_hbm, c_hi), load(2, c_lo_hbm, c_lo)]
+    later_loads = [
+        load(3, lines_hbm.at[gyi], lines), load(4, s_hi_hbm, s_hi), load(5, s_lo_hbm, s_lo),
     ]
-    for load in loads:
-        load.start()
-
-    for t in range(quads):
-        cells = [[f_ref[pl.ds(4 * t + 2 * b1 + b0, lx, stride=ly), :] for b1 in range(2)]
-                 for b0 in range(2)]
+    for copy in first_loads:
+        copy.wait()
+
+    for t in range(steps):
+        cells = [
+            [f_ref[pl.ds(2 * (t * sub + s) + b, lx, stride=ly), :] for s in range(sub)]
+            for b in range(2)
+        ]
         spread = jnp.concatenate([jnp.concatenate(row, axis=1) for row in cells], axis=0)
         high, low = split(spread)
         g_hi[t] = high
         g_lo[t] = low
-    for load in loads:
-        load.wait()
 
     def block_of(index):
         return pl.ds(pl.multiple_of(index * block, block), block)
 
     def z_forward(c):
-        for t in range(quads):
+        for t in range(steps):
             piece = product((c_hi[c], c_lo[c]), (g_hi[t], g_lo[t]), ((1,), (1,)))
             for j in range(gy):
-                out_fwd[c, j * block + t * rows : j * block + (t + 1) * rows, :] = piece[
-                    j * rows : (j + 1) * rows, :
+                out_fwd[c, j * block + t * TILE : j * block + (t + 1) * TILE, :] = piece[
+                    j * TILE : (j + 1) * TILE, :
                 ]
 
     def y_copies(c, out, into, send, recv):
@@ -184,6 +184,8 @@
         z_forward(c)
         fwd.append(exchange(c, out_fwd, in_fwd, fwd_send, fwd_recv))
 
+    for copy in later_loads:
+        copy.wait()
     for c in range(CHUNKS):
         ratio = lines[c, 0]
         power = jnp.ones_like(ratio)
@@ -197,7 +199,7 @@
         tall = []
         for m in range(group):
             cells = jnp.concatenate(
-                [in_fwd[c, pl.ds(b1 * group + m, half, stride=rows), :] for b1 in range(2)], axis=0
+                [in_fwd[c, pl.ds(s * group + m, part, stride=TILE), :] for s in range(sub)], axis=0
             ).T
             tall.append(jnp.concatenate([cells[:lx], cells[lx:]], axis=1))
         spectral = product(split(jnp.concatenate(tall, axis=0)), (s_hi[...], s_lo[...]),
@@ -231,8 +233,8 @@
             value = line(wave, c, b)
             left[b % 4] += value * powers[c, b]
             right[b % 4] += value * powers[c, lx - 1 - b]
-        ends[c, 0] = (left[0] + left[1]) + (left[2] + left[3])
-        ends[c, 1] = (right[0] + right[1]) + (right[2] + right[3])
+        ends[c, :rows] = (left[0] + left[1]) + (left[2] + left[3])
+        ends[c, rows:] = (right[0] + right[1]) + (right[2] + right[3])
         sends, arrivals = small_copies(
             c, ends, ends_x, xi, x_send, x_recv, x_order, x_peer,
             lambda d: lax.rem(xi - d + x_chips, x_chips),
@@ -258,13 +260,13 @@
         for copy in copies[1]:
             copy.wait_recv()
         span = powers[c, lx - 1] * lines[c, 0]
-        left = ends_x[c, x_chips - 1, 0]
-        right = ends_x[c, 0, 1]
+        left = ends_x[c, x_chips - 1, :rows]
+        right = ends_x[c, 0, rows:]
         for i in range(1, x_chips):
-            left = span * left + ends_x[c, x_chips - 1 - i, 0]
-            right = span * right + ends_x[c, i, 1]
-        tops[c, 0] = left
-        tops[c, 1] = right
+            left = span * left + ends_x[c, x_chips - 1 - i, :rows]
+            right = span * right + ends_x[c, i, rows:]
+        tops[c, :rows] = left
+        tops[c, rows:] = right
         sends, arrivals = small_copies(
             c, tops, tops_z, zi, z_send, z_recv, range(1, z_chips), z_peer,
             lambda d: lax.rem(zi - d + z_chips, z_chips),
@@ -274,13 +276,13 @@
         tops_z[c, zi] = tops[c]
         return sends, arrivals
 
-    def arriving(span, count, place, parts, left_start, right_start):
+    def arriving(c, span, count, place, parts, left_start, right_start):
         right = right_start
         left = left_start
         for i in range(count):
-            left = jnp.where(i < place, span * left + parts(i, 1), left)
+            left = jnp.where(i < place, span * left + parts[c, i, rows:], left)
             o = count - 1 - i
-            right = jnp.where(o > place, span * right + parts(o, 0), right)
+            right = jnp.where(o > place, span * right + parts[c, o, :rows], right)
         return left, right
 
     def x_finish(c, copies):
@@ -294,16 +296,16 @@
             whole = whole * wide
         for copy in copies[1]:
             copy.wait_recv()
-        left = tops_z[c, z_chips - 1, 0]
-        right = tops_z[c, 0, 1]
+        left = tops_z[c, z_chips - 1, :rows]
+        right = tops_z[c, 0, rows:]
         for i in range(1, z_chips):
-            left = wide * left + tops_z[c, z_chips - 1 - i, 0]
-            right = wide * right + tops_z[c, i, 1]
+            left = wide * left + tops_z[c, z_chips - 1 - i, :rows]
+            right = wide * right + tops_z[c, i, rows:]
         closing = 1.0 / (1.0 - whole * whole)
         first = (left + whole * right) * closing
         last = (right + whole * left) * closing
-        first, last = arriving(wide, z_chips, zi, lambda i, s: tops_z[c, i, s], first, last)
-        first, last = arriving(span, x_chips, xi, lambda i, s: ends_x[c, i, s], first, last)
+        first, last = arriving(c, wide, z_chips, zi, tops_z, first, last)
+        first, last = arriving(c, span, x_chips, xi, ends_x, first, last)
         first = first * (ratio * scale)
         last = last * (ratio * scale)
         for b in range(lx):
@@ -318,20 +320,20 @@
         lanes = jnp.concatenate([solved[c, h * flat : (h + 1) * flat, :] for h in range(2)], axis=1)
         cells = product(split(lanes), (s_hi[...], s_lo[...]), ((1,), (1,)))
         for m in range(group):
-            part = cells[m * lx : (m + 1) * lx]
-            part = jnp.concatenate([part[:, : ny // 2], part[:, ny // 2 :]], axis=0).T
-            for b1 in range(2):
-                out_bwd[c, pl.ds(b1 * group + m, half, stride=rows), :] = part[
-                    b1 * half : (b1 + 1) * half
+            wide = cells[m * lx : (m + 1) * lx]
+            tall = jnp.concatenate([wide[:, : ny // 2], wide[:, ny // 2 :]], axis=0).T
+            for s in range(sub):
+                out_bwd[c, pl.ds(s * group + m, part, stride=TILE), :] = tall[
+                    s * part : (s + 1) * part
                 ]
         return exchange(c, out_bwd, in_bwd, bwd_send, bwd_recv)
 
     def z_backward(c, copies):
         for copy in copies[1]:
             copy.wait_recv()
-        for t in range(quads):
+        for t in range(steps):
             waves = jnp.concatenate(
-                [in_bwd[c, j * block + t * rows : j * block + (t + 1) * rows, :]
+                [in_bwd[c, j * block + t * TILE : j * block + (t + 1) * TILE, :]
                  for j in range(gy)], axis=0,
             ).T
             cells = product(split(waves), (c_hi[c], c_lo[c]), ((1,), (0,)))
@@ -340,28 +342,36 @@
             if c < CHUNKS - 1:
                 total[t] = cells
             else:
-                for b0 in range(2):
-                    for b1 in range(2):
-                        o_ref[pl.ds(4 * t + 2 * b1 + b0, lx, stride=ly), :] = cells[
-                            b0 * lx : (b0 + 1) * lx, b1 * nz : (b1 + 1) * nz
+                for b in range(2):
+                    for s in range(sub):
+                        o_ref[pl.ds(2 * (t * sub + s) + b, lx, stride=ly), :] = cells[
+                            b * lx : (b + 1) * lx, s * nz : (s + 1) * nz
                         ]
 
-    assert CHUNKS == 2
-    y_forward(0)
-    x_copies = [x_ends(0)]
-    x_local(0)
-    y_forward(1)
-    x_copies.append(x_ends(1))
-    z_copies = [x_group(0, x_copies[0])]
-    x_local(1)
-    x_finish(0, z_copies[0])
-    bwd = [y_backward(0)]
-    z_copies.append(x_group(1, x_copies[1]))
-    x_finish(1, z_copies[1])
-    bwd.append(y_backward(1))
-    z_backward(0, bwd[0])
-    z_backward(1, bwd[1])
-    for sends, _ in fwd + x_copies + z_copies + bwd:
+    x_copies, z_copies, bwd = {}, {}, {}
+
+    def lines_out(c):
+        y_forward(c)
+        x_copies[c] = x_ends(c)
+        x_local(c)
+
+    def tops_out(c):
+        z_copies[c] = x_group(c, x_copies[c])
+
+    def back_out(c):
+        x_finish(c, z_copies[c])
+        bwd[c] = y_backward(c)
+
+    for slot in range(CHUNKS + 3):
+        if slot < CHUNKS:
+            lines_out(slot)
+        if 0 <= slot - 1 < CHUNKS:
+            tops_out(slot - 1)
+        if 0 <= slot - 2 < CHUNKS:
+            back_out(slot - 2)
+    for c in range(CHUNKS):
+        z_backward(c, bwd[c])
+    for sends, _ in [*fwd, *x_copies.values(), *z_copies.values(), *bwd.values()]:
         for copy in sends:
             copy.wait_send()
 
@@ -371,36 +381,38 @@
     ny = ly * gy
     z_chips = gx // x_chips
     group = nz // gy // CHUNKS
+    sub = TILE // group
+    steps = ly // (2 * sub)
     rows, ql = 2 * group, ny // 2
     c_hi, c_lo = z_tables(nz, gy)
-    s_hi, s_lo = y_tables(ny, gy)
+    s_hi, s_lo = y_tables(ny, gy, sub)
     lines = line_tables(ny, nz, gy)
-    buffer = pltpu.VMEM((CHUNKS, gy * (ly // 4) * rows, 2 * lx), f32)
+    buffer = pltpu.VMEM((CHUNKS, gy * steps * TILE, 2 * lx), f32)
     spectral = pltpu.VMEM((CHUNKS, rows * lx, ql), f32)
     stack = pltpu.VMEM((CHUNKS, lx, rows, ql), f32)
-    quad = pltpu.VMEM((ly // 4, 2 * lx, 2 * nz), bf16)
+    cells = pltpu.VMEM((steps, 2 * lx, sub * nz), bf16)
     dma = pltpu.SemaphoreType.DMA
     scratch = [
+        pltpu.VMEM((lx * ly, nz), f32),
         pltpu.VMEM(c_hi.shape, bf16), pltpu.VMEM(c_lo.shape, bf16),
         pltpu.VMEM(s_hi.shape, bf16), pltpu.VMEM(s_lo.shape, bf16),
         pltpu.VMEM(lines.shape[1:], f32),
-        quad, quad, buffer, buffer, spectral, stack, stack, stack, spectral, buffer, buffer,
-        pltpu.VMEM((ly // 4, 2 * lx, 2 * nz), f32),
-        pltpu.VMEM((CHUNKS, 2, rows, ql), f32),
-        pltpu.VMEM((CHUNKS, x_chips, 2, rows, ql), f32),
-        pltpu.VMEM((CHUNKS, 2, rows, ql), f32),
-        pltpu.VMEM((CHUNKS, z_chips, 2, rows, ql), f32),
-        dma((5,)),
+        cells, cells, buffer, buffer, spectral, stack, stack, stack, spectral, buffer, buffer,
+        pltpu.VMEM((steps, 2 * lx, sub * nz), f32),
+        pltpu.VMEM((CHUNKS, 2 * rows, ql), f32),
+        pltpu.VMEM((CHUNKS, x_chips, 2 * rows, ql), f32),
+        pltpu.VMEM((CHUNKS, 2 * rows, ql), f32),
+        pltpu.VMEM((CHUNKS, z_chips, 2 * rows, ql), f32),
+        dma((6,)),
         dma((CHUNKS, gy - 1)), dma((CHUNKS, gy - 1)), dma((CHUNKS, gy - 1)), dma((CHUNKS, gy - 1)),
         dma((CHUNKS, x_chips - 1)), dma((CHUNKS, x_chips - 1)),
         dma((CHUNKS, z_chips - 1)), dma((CHUNKS, z_chips - 1)),
     ]
-    vmem, anywhere = pl.BlockSpec(memory_space=pltpu.VMEM), pl.BlockSpec(memory_space=pl.ANY)
     pressure = pl.pallas_call(
         functools.partial(kernel, gx, gy, x_chips, lx, ly, nz, ny),
-        out_shape=jax.ShapeDtypeStruct((lx * ly, nz), f32),
-        in_specs=[vmem] + [anywhere] * 5,
-        out_specs=vmem,
+        out_shape=pltpu.VMEM((lx * ly, nz), f32),
+        in_specs=[pl.BlockSpec(memory_space=pl.ANY)] * 6,
+        out_specs=pl.BlockSpec(memory_space=pltpu.VMEM),
         scratch_shapes=scratch,
         compiler_params=pltpu.CompilerParams(collective_id=0, has_side_effects=True),
     )(source.reshape(lx * ly, nz), c_hi, c_lo, s_hi, s_lo, lines)

time: 53.2 us -> 48.3 us (0.908)
  Pallas kernels: 51.1 us -> 47.4 us
  local copies, waits for them, and re-layouts: 1.87 us -> 0.8 us
    pallas_call x1, Pallas kernels: 51.1 us -> 47.4 us  [solve(): pl.pallas_call(functools.partial(kernel, gx, gy, x_chips, lx, ly, nz, ny)...]
    unnamed x1, local copies, waits for them, and re-layouts: 1.87 us -> 0.8 us
where the time goes in v2:
time: 48.3 us; the launch traced here: 48.2 us
  Pallas kernels  47.4 us (98%)
  local copies, waits for them, and re-layouts  0.8 us (2%)
    pallas_call x1, Pallas kernels, solve(): pl.pallas_call(functools.partial(kernel, gx, gy, x_chips, lx, ly, nz, ny)...  47.4 us

profile of v2, /device:TPU:1, one launch (start us, length us, event | category | flops | bytes accessed | tf_op | source)
XLA Modules:
  0.0 48.2 jit_solution(7773862416421916770)
XLA Ops:
  0.0 47.4 %shard_map.64 = f32[1024,128]{1,0:T(8,128)S(1)} custom-call(f32[1024,128]{1,0:T(8,128)} %bitcast.3, bf16[4,128,512]{2,1,0:T(8,128)(2,1)} %constant.10.clone.c_hi_hbm, bf16[4,128,512]{2,1,0:T(8,128)(2,1)} %constant.11.clone.c_lo_hbm, bf16[256,256]{1,0:T(8,128)(2,1)} %constant.12.clone.s_hi_hbm, bf16[256,256]{1,0:T(8,128)(2,1)} %constant.13.clone.s_lo_hbm, ...), custom_call_target="tpu_custom_call" | custom-call | tf_op jit(solution)/shard_map/pallas_call | solution.py:411
  47.4 0.8 %copy.8 = f32[64,16,128]{2,1,0:T(8,128)} copy(f32[64,16,128]{2,1,0:T(8,128)S(1)} %bitcast.2) | data formatting | bytes 1048576

commit v3 on v2

--- a/solution.py
+++ b/solution.py
@@ -11,7 +11,7 @@
 from jax.sharding import PartitionSpec as P
 
 SCREEN = 32
-X_CHIPS = 8
+X_CHIPS = 4
 CHUNKS = 4
 TILE = 8
 MESH = pl.DeviceIdType.MESH

time: 48.3 us -> 47.7 us (0.988)
  Pallas kernels: 47.4 us -> 46.8 us
    pallas_call x1, Pallas kernels: 47.4 us -> 46.8 us  [solve(): pl.pallas_call(functools.partial(kernel, gx, gy, x_chips, lx, ly, nz, ny)...]
where the time goes in v3:
time: 47.7 us; the launch traced here: 47.6 us
  Pallas kernels  46.8 us (98%)
  local copies, waits for them, and re-layouts  0.8 us (2%)
    pallas_call x1, Pallas kernels, solve(): pl.pallas_call(functools.partial(kernel, gx, gy, x_chips, lx, ly, nz, ny)...  46.8 us

profile of v3, /device:TPU:1, one launch (start us, length us, event | category | flops | bytes accessed | tf_op | source)
XLA Modules:
  0.0 47.6 jit_solution(1102101711254077591)
XLA Ops:
  0.0 46.8 %shard_map.64 = f32[1024,128]{1,0:T(8,128)S(1)} custom-call(f32[1024,128]{1,0:T(8,128)} %bitcast.3, bf16[4,128,512]{2,1,0:T(8,128)(2,1)} %constant.10.clone.c_hi_hbm, bf16[4,128,512]{2,1,0:T(8,128)(2,1)} %constant.11.clone.c_lo_hbm, bf16[256,256]{1,0:T(8,128)(2,1)} %constant.12.clone.s_hi_hbm, bf16[256,256]{1,0:T(8,128)(2,1)} %constant.13.clone.s_lo_hbm, ...), custom_call_target="tpu_custom_call" | custom-call | tf_op jit(solution)/shard_map/pallas_call | solution.py:411
  46.8 0.8 %copy.8 = f32[64,16,128]{2,1,0:T(8,128)} copy(f32[64,16,128]{2,1,0:T(8,128)S(1)} %bitcast.2) | data formatting | bytes 1048576
